TPU v7x, 128 devices: a whole 4x4x4 slice. The times are simulated.
128 devices in a mesh: req: 8 (over y, core), exp: 16 (over z, x).
Axes of the slice: x: 4, y: 4, z: 4, core: 2. Of those that a mesh axis runs over, the one named last changes fastest.
Arguments:
- resid: bfloat16 [8192, 2048], P(('req', 'exp')), may hold values from -27 to 27
- queries: bfloat16 [8192, 2048], P(('req', 'exp')), may hold values from -6 to 6
- cache_key: bfloat16 [256, 128, 2048], P(('req', 'exp')), may hold values from -6 to 6
- cache_value: bfloat16 [256, 128, 2048], P(('req', 'exp')), may hold values from -6 to 6
- page_table: int32 [32, 8], P('req'), may hold values from 0 to 31, as said below
- row_request: int32 [8192], P('req'), may hold values from 0 to 3, as said below
- row_position: int32 [8192], P('req'), may hold values from 0 to 1023, as said below
- out_proj: bfloat16 [2048, 2048], P('exp'), may hold values from -0.375 to 0.375
- norm_gain: float32 [2048], replicated, may hold values from 0.5 to 1.5
- expert_gate: bfloat16 [128, 2048, 1408], P(('req', 'exp')), as said below
- expert_up: bfloat16 [128, 2048, 1408], P(('req', 'exp')), as said below
- expert_down: bfloat16 [128, 1408, 2048], P(('req', 'exp')), as said below
- shared_gate: bfloat16 [2048, 5632], P(None, 'exp'), may hold values from -0.125 to 0.125
- shared_up: bfloat16 [2048, 5632], P(None, 'exp'), may hold values from -0.125 to 0.125
- shared_down: bfloat16 [5632, 2048], P('exp'), may hold values from -0.078125 to 0.078125
- shared_scalar: bfloat16 [2048], replicated, may hold values from -0.375 to 0.375
- slot_expert: int32 [128], replicated, may hold values from 0 to 59, as said below
- route_expert: int32 [8192, 4], replicated, may hold values from 0 to 59, as said below
- route_gate: float32 [8192, 4], P(('req', 'exp')), may hold values from 0.05 to 0.5
Outputs:
- output: bfloat16 [8192, 2048], P(('req', 'exp'))
Inputs may be any that keep to these rules, and one draw needn't show every extreme that they name: `page_table`: within each request group the table names each of the group's 32 pages once; page p of group g lies on the device of req index g and exp index p // 2. `row_request`: each group's rows are in order of request; every request has one row or more; half of the requests of a group have exactly one row. `row_position`: the rows of one request hold consecutive positions ending at the request's length minus one. `slot_expert`: every expert is held by one slot or more. `route_expert`: each row names 4 different experts. In each aligned block of 64 rows (the rows of one device) no expert is named more than 6 times, and one expert is named exactly 6 times in every block. `expert_gate`: slots that hold the same expert hold equal weights. `expert_up`: slots that hold the same expert hold equal weights. `expert_down`: slots that hold the same expert hold equal weights.
All inputs are finite; a program needn't handle non-finite values.
Results may differ from a plain program's by a relative error of at most 0.006.
Values may be sent and summed in bfloat16 or wider, within the bound.
A program may use at most 128 MiB of HBM per device.

v0:
```python
import math

import jax
import jax.numpy as jnp
from jax import lax
from jax.sharding import PartitionSpec as P

HEADS = 16
HEAD_DIM = 128
TOPK = 4


def expert_block(rows, gate_w, up_w, down_w):
    gate = jnp.dot(rows, gate_w, preferred_element_type=jnp.float32)
    upper = jnp.dot(rows, up_w, preferred_element_type=jnp.float32)
    hidden = (jax.nn.silu(gate) * upper).astype(jnp.bfloat16)
    return jnp.dot(hidden, down_w, preferred_element_type=jnp.float32).astype(jnp.bfloat16)


def rms_normed(stream, norm_gain):
    scale_row = lax.rsqrt(jnp.mean(stream * stream, axis=1, keepdims=True) + 1e-06)
    return (stream * scale_row * norm_gain[None, :]).astype(jnp.bfloat16)


def shards(
    resid,
    queries,
    cache_key,
    cache_value,
    page_table,
    row_request,
    row_position,
    out_proj,
    norm_gain,
    expert_gate,
    expert_up,
    expert_down,
    shared_gate,
    shared_up,
    shared_down,
    shared_scalar,
    slot_expert,
    route_expert,
    route_gate,
):
    exp_count = lax.axis_size("exp")
    req_count = lax.axis_size("req")
    slot_count = exp_count * req_count
    exp_index = lax.axis_index("exp")
    own_slot = lax.axis_index("req") * exp_count + exp_index
    tok_rows = resid.shape[0]
    model_width = resid.shape[1]
    group_rows = row_request.shape[0]
    pages_here = cache_key.shape[0]
    page_len = cache_key.shape[1]
    req_slots = page_table.shape[0]
    max_pages = page_table.shape[1]
    capacity = 3 * tok_rows * TOPK // slot_count
    whole_queries = lax.all_gather(queries, "exp", axis=0, tiled=True)
    page_ids = exp_index * pages_here + jnp.arange(pages_here, dtype=jnp.int32)
    hits = (page_table[None, :, :] == page_ids[:, None, None]).astype(jnp.int32)
    page_request = jnp.sum(
        hits * jnp.arange(req_slots, dtype=jnp.int32)[None, :, None], axis=(1, 2)
    )
    page_slot = jnp.sum(hits * jnp.arange(max_pages, dtype=jnp.int32)[None, None, :], axis=(1, 2))
    key_position = (
        page_slot[:, None] * page_len + jnp.arange(page_len, dtype=jnp.int32)[None, :]
    ).reshape(-1)
    key_request = jnp.repeat(page_request, page_len)
    visible = (row_request[:, None] == key_request[None, :]) & (
        key_position[None, :] <= row_position[:, None]
    )
    key_count = pages_here * page_len
    query_heads = whole_queries.reshape(group_rows, HEADS, HEAD_DIM)
    key_heads = cache_key.reshape(key_count, HEADS, HEAD_DIM)
    value_heads = cache_value.reshape(key_count, HEADS, HEAD_DIM)
    scores = jnp.einsum(
        "rhd,khd->hrk", query_heads, key_heads, preferred_element_type=jnp.float32
    ) * HEAD_DIM ** (-0.5)
    scores = jnp.where(visible[None], scores, -1e30)
    top = lax.pmax(jnp.max(scores, axis=2), "exp")
    weights = jnp.where(visible[None], jnp.exp(scores - top[:, :, None]), 0.0)
    denominators = jnp.transpose(jnp.sum(weights, axis=2))
    numerators = jnp.einsum(
        "hrk,khd->rhd",
        weights.astype(jnp.bfloat16),
        value_heads,
        preferred_element_type=jnp.float32,
    ).reshape(group_rows, model_width)
    num_cols, den_cols = (
        lax.psum_scatter(numerators, "exp", scatter_dimension=1, tiled=True),
        lax.psum_scatter(denominators, "exp", scatter_dimension=1, tiled=True),
    )
    local_heads = den_cols.shape[1]
    attention = (
        (num_cols.reshape(group_rows, local_heads, HEAD_DIM) / den_cols[:, :, None])
        .reshape(group_rows, local_heads * HEAD_DIM)
        .astype(jnp.bfloat16)
    )
    mixed = lax.psum_scatter(
        jnp.dot(attention, out_proj, preferred_element_type=jnp.float32),
        "exp",
        scatter_dimension=0,
        tiled=True,
    )
    stream = resid.astype(jnp.float32) + mixed
    normed = rms_normed(stream, norm_gain)
    piece = lax.all_gather(normed, "exp", axis=0, tiled=True)
    gate = jnp.dot(piece, shared_gate, preferred_element_type=jnp.float32)
    upper = jnp.dot(piece, shared_up, preferred_element_type=jnp.float32)
    shared_hidden = (jax.nn.silu(gate) * upper).astype(jnp.bfloat16)
    shared_out = lax.psum_scatter(
        jnp.dot(shared_hidden, shared_down, preferred_element_type=jnp.float32).astype(
            jnp.bfloat16
        ),
        "exp",
        scatter_dimension=0,
        tiled=True,
    ).astype(jnp.float32)
    shared_scale = jax.nn.sigmoid(
        jnp.dot(normed, shared_scalar, preferred_element_type=jnp.float32)
    )
    slot_ids = jnp.arange(slot_count, dtype=jnp.int32)
    same_expert = slot_expert[:, None] == slot_expert[None, :]
    copy_rank = jnp.sum(
        (same_expert & (slot_ids[None, :] < slot_ids[:, None])).astype(jnp.int32), axis=1
    )
    own_routes = lax.dynamic_slice_in_dim(route_expert, own_slot * tok_rows, tok_rows, 0).reshape(
        -1
    )
    holds = own_routes[:, None] == slot_expert[None, :]
    copy_total = jnp.sum(holds.astype(jnp.int32), axis=1)
    own_mark = slot_ids == own_slot
    own_expert = jnp.sum(jnp.where(own_mark, slot_expert, 0))
    own_rank = jnp.sum(jnp.where(own_mark, copy_rank, 0))
    wanted = jnp.zeros_like(copy_total)
    taken = jnp.broadcast_to(own_rank == 0, (slot_count,))
    chosen = holds & (copy_rank[None, :] == wanted[:, None])
    target = jnp.sum(jnp.where(chosen, slot_ids[None, :], 0), axis=1)
    onehot = chosen.astype(jnp.int32)
    position = jnp.sum(jnp.cumsum(onehot, axis=0) * onehot, axis=1) - 1
    buffer_index = target * capacity + position
    entry_rows = jnp.repeat(normed, TOPK, axis=0)
    outgoing = (
        jnp.zeros((slot_count * capacity, model_width), jnp.bfloat16)
        .at[buffer_index]
        .set(entry_rows)
    )
    outgoing = outgoing.reshape(slot_count, capacity, model_width)
    named = (
        jnp.sum((route_expert == own_expert).astype(jnp.int32), axis=1)
        .reshape(slot_count, tok_rows)
        .sum(axis=1)
    )
    arrived = jnp.where(taken, named, 0)
    incoming = lax.all_to_all(outgoing, ("req", "exp"), split_axis=0, concat_axis=0, tiled=True)
    filled = (jnp.arange(capacity, dtype=jnp.int32)[None, :] < arrived[:, None]).reshape(-1)
    packed_order = jnp.argsort(1 - filled.astype(jnp.int32), stable=True)
    packed = incoming.reshape(-1, model_width)[packed_order]
    live = jnp.sum(filled.astype(jnp.int32))
    tile = math.gcd(128, slot_count * capacity)

    def tile_step(step, results):
        rows = lax.dynamic_slice_in_dim(packed, step * tile, tile, 0)
        answer = expert_block(rows, expert_gate[0], expert_up[0], expert_down[0])
        return lax.dynamic_update_slice_in_dim(results, answer, step * tile, 0)

    results = lax.fori_loop(0, (live + tile - 1) // tile, tile_step, jnp.zeros_like(packed))
    answered = (
        jnp.zeros_like(results)
        .at[packed_order]
        .set(results)
        .reshape(slot_count, capacity, model_width)
    )
    returned = lax.all_to_all(
        answered, ("req", "exp"), split_axis=0, concat_axis=0, tiled=True
    ).reshape(-1, model_width)
    expert_out = returned[buffer_index].reshape(tok_rows, TOPK, model_width)
    routed = jnp.sum(expert_out.astype(jnp.float32) * route_gate[:, :, None], axis=1)
    return (stream + shared_scale[:, None] * shared_out + routed).astype(jnp.bfloat16)


def solution(mesh):
    placed = (
        P(("req", "exp"), None),
        P(("req", "exp"), None),
        P(("req", "exp"), None, None),
        P(("req", "exp"), None, None),
        P("req", None),
        P("req"),
        P("req"),
        P("exp", None),
        P(),
        P(("req", "exp"), None, None),
        P(("req", "exp"), None, None),
        P(("req", "exp"), None, None),
        P(None, "exp"),
        P(None, "exp"),
        P("exp", None),
        P(),
        P(),
        P(),
        P(("req", "exp"), None),
    )
    return jax.shard_map(
        shards, mesh=mesh, in_specs=placed, out_specs=P(("req", "exp"), None), check_vma=False
    )
```

profile of v0, /device:TPU:0, one launch (start us, length us, event | category | flops | bytes accessed | tf_op | source)
XLA Modules:
  0.0 703.1 jit_solution(17260760574157700612)
XLA Ops:
  6.5 0.7 all-gather.3.cloned.1.call-update
  7.3 1.4 copy.57
  8.8 0.9 fusion.59
  9.8 1.0 compare_and_fusion
  10.8 52.9 %all-gather.3.cloned.1.call-done = bf16[1024,2048]{1,0:T(8,128)(2,1)} async-done(((bf16[64,2048]{1,0:T(8,128)(2,1)}), bf16[1024,2048]{1,0:T(8,128)(2,1)}) %all-gather.3.cloned.1.call-update) | async-done | bytes 4194320 | tf_op jit(solution)/shard_map/all_gather | solution.py:59
  63.7 6.4 copy.44
  70.1 10.7 %fusion.28 = (f32[16,1024]{1,0:T(8,128)}, f32[16,1024,256]{1,2,0:T(8,128)}) fusion(pred[1024,256]{0,1:T(8,128)(4,1)S(1)} %compare_and_fusion, bf16[1024,16,128]{0,2,1:T(8,128)(2,1)} %bitcast.74, bf16[256,16,128]{2,1,0:T(8,128)(2,1)S(1)} %bitcast.75), kind=kOutput, calls=%fused_computation.22 | convolution fusion | flops 1086308352 | bytes 22347776 | tf_op jit(solution)/shard_map/rhd,khd->hrk/dot_general | solution.py:77
  80.8 1.5 copy.56
  82.3 79.2 %all-reduce.4.cloned.1.call-done = f32[16,1024]{1,0:T(8,128)} async-done(((f32[16,1024]{1,0:T(8,128)}), f32[16,1024]{1,0:T(8,128)}) %all-reduce.4.cloned.1.call-update) | async-done | bytes 65552 | tf_op jit(solution)/shard_map/pmax | solution.py:81
  161.5 8.6 %fusion.29 = f32[16,1024]{1,0:T(8,128)} fusion(f32[16,1024,256]{1,2,0:T(8,128)} %get-tuple-element.67, f32[16,1024]{1,0:T(8,128)} %all-reduce.4.cloned.1.call-done, pred[1024,256]{0,1:T(8,128)(4,1)S(1)} %compare_and_fusion), kind=kLoop, calls=%fused_computation.23 | loop fusion | flops 20955136 | bytes 17170432 | tf_op jit(solution)/shard_map/reduce_sum | solution.py:83
  170.2 13.6 %fusion.31 = f32[16,1024,128]{1,2,0:T(8,128)} fusion(f32[16,1024,256]{1,2,0:T(8,128)} %get-tuple-element.67, f32[16,1024]{1,0:T(8,128)S(1)} %copy-done.6, pred[1024,256]{0,1:T(8,128)(4,1)S(1)} %compare_and_fusion, bf16[256,16,128]{2,1,0:T(8,128)(2,1)S(1)} %bitcast.79), kind=kOutput, calls=%fused_computation.25 | convolution fusion | flops 1094713344 | bytes 26542080 | tf_op jit(solution)/shard_map/hrk,khd->rhd/dot_general | solution.py:84
  183.9 0.6 copy-done.12
  184.5 0.6 dynamic-slice
  185.1 65.4 %all-reduce.6.cloned.1.call-done = f32[1024,16]{0,1:T(8,128)} async-done(((f32[1024,16]{0,1:T(8,128)}), f32[1024,16]{0,1:T(8,128)}) %all-reduce.6.cloned.1.call-update) | async-done | bytes 65552
  250.5 1.4 constant_dynamic-slice_fusion
  251.9 86.1 %reduce-scatter.4.cloned.1.call-done = f32[1024,128]{0,1:T(8,128)} async-done(((f32[1024,2048]{0,1:T(8,128)}), f32[1024,128]{0,1:T(8,128)}) %reduce-scatter.4.cloned.1.call-update) | async-done | bytes 524304 | tf_op jit(solution)/shard_map/reduce_scatter | solution.py:91
  338.0 5.5 fusion.51
  343.6 11.0 %all-gather.5.cloned.1.call-start = ((), (), s32[]{:S(2)}) async-start(), calls=%async_computation.9 | async-start | bytes 4456448 | tf_op jit(solution)/shard_map/all_gather | solution.py:108
  354.6 73.5 %reduce-scatter.6.cloned.1.call-done = f32[64,2048]{1,0:T(8,128)} async-done(((f32[1024,2048]{1,0:T(8,128)}), f32[64,2048]{1,0:T(8,128)}) %reduce-scatter.6.cloned.1.call-update) | async-done | bytes 524304 | tf_op jit(solution)/shard_map/reduce_scatter | solution.py:100
  428.1 1.2 multiply_reduce_fusion.1
  429.4 1.9 multiply_convert_fusion
  431.3 0.8 constant_dynamic-slice_fusion.1
  432.4 0.2 convert_reduce_fusion.2
  432.6 0.2 fusion.53
  432.9 0.2 select_reduce_fusion
  433.2 1.4 broadcast_in_dim.82
  434.7 0.3 reshape.230
  434.9 4.3 scatter_custom_fusion
  439.2 6.3 reshape.205
  445.5 8.4 %all-to-all-start = ((bf16[128,6,2048]{2,1,0:T(8,128)(2,1)}), bf16[128,6,2048]{2,1,0:T(8,128)(2,1)}, u32[]{:S(2)}, u32[]{:S(2)}) async-start(bf16[128,6,2048]{2,1,0:T(8,128)(2,1)} %reshape.205), calls=%async_computation.3 | async-start | bytes 8388608 | tf_op jit(solution)/shard_map/all_to_all | solution.py:156
  454.0 0.7 fusion.61
  454.7 0.8 convert_reduce_fusion
  455.6 0.1 reduce_sum.125
  456.3 0.7 convert_reduce_fusion.1
  457.6 0.1 sub.32
  457.8 4.4 sort.17
  462.1 55.2 %all-gather.5.cloned.1.call-done = bf16[1024,2048]{1,0:T(8,128)(2,1)} async-done(((bf16[64,2048]{1,0:T(8,128)(2,1)}), bf16[1024,2048]{1,0:T(8,128)(2,1)}) %all-gather.5.cloned.1.call-update) | async-done | bytes 4194320 | tf_op jit(solution)/shard_map/all_gather | solution.py:108
  517.3 5.0 fusion.67
  522.3 8.9 %convolution_convert_fusion = bf16[1024,2048]{1,0:T(8,128)(2,1)} fusion(bf16[352,2048]{1,0:T(8,128)(2,1)S(1)} %copy-done, bf16[1024,2048]{1,0:T(8,128)(2,1)} %all-gather.5.cloned.1.call-done, bf16[2048,352]{0,1:T(8,128)(2,1)} %param.34, f32[1024,352]{0,1:T(8,128)} %fusion.67), kind=kOutput, calls=%fused_computation.31 | convolution fusion | flops 2957049856 | bytes 12713984 | tf_op jit(solution)/shard_map/dot_general | solution.py:113
  531.3 4.9 reshape.206
  536.2 4.3 gather_fusion
  540.5 2.1 broadcast.171
  542.6 56.4 %while.10 = (s32[]{:T(128)}, bf16[768,2048]{1,0:T(8,128)(2,1)}, s32[]{:T(128)}, bf16[768,2048]{1,0:T(8,128)(2,1)}, bf16[1,2048,1408]{2,1,0:T(8,128)(2,1)}, /*ind...) while((s32[]{:T(128)}, bf16[768,2048]{1,0:T(8,128)(2,1)}, ...), condition=%wide.region_23.24_spmd, body=%wide.region_22.23_spmd.sunk | while | flops 2215936000 | bytes 20317344 | solution.py:168
  542.6 3.8 fusion.89
  546.4 7.3 %fusion.90 = bf16[768,2048]{1,0:T(8,128)(2,1)} fusion(bf16[768,2048]{1,0:T(8,128)(2,1)} %get-tuple-element.128, s32[]{:T(128)S(6)} %select_n.89, bf16[1,1408,2048]{2,1,0:T(8,128)(2,1)} %get-tuple-element.144, bf16[1,2048,1408]{2,1,0:T(8,128)(2,1)} %get-tuple-element.143, f32[128,1408]{1,0:T(8,128)S(1)} %fusion.89, ...), kind=kOutput, calls=%fused_computation.13.clone.1 | convolution fusion | flops 1477738496 | bytes 13304832 | tf_op jit(solution)/shard_map/while/body/dot_general | solution.py:17
  553.7 4.1 fusion.89
  557.7 7.3 %fusion.90 = bf16[768,2048]{1,0:T(8,128)(2,1)} fusion(bf16[768,2048]{1,0:T(8,128)(2,1)} %get-tuple-element.128, s32[]{:T(128)S(6)} %select_n.89, bf16[1,1408,2048]{2,1,0:T(8,128)(2,1)} %get-tuple-element.144, bf16[1,2048,1408]{2,1,0:T(8,128)(2,1)} %get-tuple-element.143, f32[128,1408]{1,0:T(8,128)S(1)} %fusion.89, ...), kind=kOutput, calls=%fused_computation.13.clone.1 | convolution fusion | flops 1477738496 | bytes 13304832 | tf_op jit(solution)/shard_map/while/body/dot_general | solution.py:17
  565.1 4.0 fusion.89
  569.1 7.3 %fusion.90 = bf16[768,2048]{1,0:T(8,128)(2,1)} fusion(bf16[768,2048]{1,0:T(8,128)(2,1)} %get-tuple-element.128, s32[]{:T(128)S(6)} %select_n.89, bf16[1,1408,2048]{2,1,0:T(8,128)(2,1)} %get-tuple-element.144, bf16[1,2048,1408]{2,1,0:T(8,128)(2,1)} %get-tuple-element.143, f32[128,1408]{1,0:T(8,128)S(1)} %fusion.89, ...), kind=kOutput, calls=%fused_computation.13.clone.1 | convolution fusion | flops 1477738496 | bytes 13304832 | tf_op jit(solution)/shard_map/while/body/dot_general | solution.py:17
  576.5 4.0 fusion.89
  580.5 7.4 %fusion.90 = bf16[768,2048]{1,0:T(8,128)(2,1)} fusion(bf16[768,2048]{1,0:T(8,128)(2,1)} %get-tuple-element.128, s32[]{:T(128)S(6)} %select_n.89, bf16[1,1408,2048]{2,1,0:T(8,128)(2,1)} %get-tuple-element.144, bf16[1,2048,1408]{2,1,0:T(8,128)(2,1)} %get-tuple-element.143, f32[128,1408]{1,0:T(8,128)S(1)} %fusion.89, ...), kind=kOutput, calls=%fused_computation.13.clone.1 | convolution fusion | flops 1477738496 | bytes 13304832 | tf_op jit(solution)/shard_map/while/body/dot_general | solution.py:17
  587.9 3.9 fusion.89
  591.8 7.2 %fusion.90 = bf16[768,2048]{1,0:T(8,128)(2,1)} fusion(bf16[768,2048]{1,0:T(8,128)(2,1)} %get-tuple-element.128, s32[]{:T(128)S(6)} %select_n.89, bf16[1,1408,2048]{2,1,0:T(8,128)(2,1)} %get-tuple-element.144, bf16[1,2048,1408]{2,1,0:T(8,128)(2,1)} %get-tuple-element.143, f32[128,1408]{1,0:T(8,128)S(1)} %fusion.89, ...), kind=kOutput, calls=%fused_computation.13.clone.1 | convolution fusion | flops 1477738496 | bytes 13304832 | tf_op jit(solution)/shard_map/while/body/dot_general | solution.py:17
  599.0 8.8 %scatter_custom_fusion.1 = bf16[768,2048]{1,0:T(8,128)(2,1)S(1)} fusion(s32[768]{0:T(1024)S(1)} %compare_select_fusion, bf16[768,2048]{1,0:T(8,128)(2,1)} %get-tuple-element.45, bf16[]{:T(256)} %constant.74.clone.1), kind=kCustom, calls=%fused_computation.33 | custom fusion | bytes 3146240 | tf_op jit(solution)/shard_map/scatter | solution.py:172
  607.8 2.9 reshape.207
  610.8 15.3 %all-to-all-start.1 = ((bf16[128,6,2048]{2,1,0:T(8,128)(2,1)}), bf16[128,6,2048]{2,1,0:T(8,128)(2,1)}, u32[]{:S(2)}, u32[]{:S(2)}) async-start(bf16[128,6,2048]{2,1,0:T(8,128)(2,1)} %reshape.207), calls=%async_computation.4 | async-start | bytes 8388608 | tf_op jit(solution)/shard_map/all_to_all | solution.py:175
  626.1 0.7 copy.53
  626.8 0.2 fusion.46
  627.0 49.8 %all-to-all-done.1 = bf16[128,6,2048]{2,1,0:T(8,128)(2,1)} async-done(((bf16[128,6,2048]{2,1,0:T(8,128)(2,1)}), bf16[128,6,2048]{2,1,0:T(8,128)(2,1)}, u32[]{:S(2)}, u32[]{:S(2)}) %all-to-all-start.1) | async-done | bytes 3145760 | tf_op jit(solution)/shard_map/all_to_all | solution.py:175
  676.8 6.3 reshape.208
  683.1 5.7 gather_fusion.1
  688.8 1.7 reshape.209
  690.6 3.1 multiply_reduce_fusion
  693.7 2.2 add_convert_fusion
  (63 shorter events, 1.1 us)
Async XLA Ops:
  6.5 515.8 %copy-start = (bf16[352,2048]{1,0:T(8,128)(2,1)S(1)}, bf16[352,2048]{1,0:T(8,128)(2,1)}, u32[]{:S(2)}) copy-start(bf16[352,2048]{1,0:T(8,128)(2,1)} %param.35) | copy-start | bytes 4325380
  6.5 57.1 %all-gather.3.cloned.1.call-start = ((), (), s32[]{:S(2)}) async-start(), calls=%async_computation.5 | async-start | bytes 4456448 | tf_op jit(solution)/shard_map/all_gather | solution.py:59
  7.3 154.2 %all-reduce.4.cloned.1.call-start = ((), (), s32[]{:S(2)}) async-start(), calls=%async_computation.6 | async-start | bytes 131072 | tf_op jit(solution)/shard_map/pmax | solution.py:81
  80.8 169.7 %all-reduce.6.cloned.1.call-start = ((), (), s32[]{:S(2)}) async-start(), calls=%async_computation.11 | async-start | bytes 131072
  161.5 8.7 %copy-start.6 = (f32[16,1024]{1,0:T(8,128)S(1)}, f32[16,1024]{1,0:T(8,128)}, u32[]{:S(2)}) copy-start(f32[16,1024]{1,0:T(8,128)} %all-reduce.4.cloned.1.call-done) | copy-start | bytes 196612
  170.2 167.9 %reduce-scatter.4.cloned.1.call-start = ((), (), s32[]{:S(2)}) async-start(), calls=%async_computation.7 | async-start | bytes 8912896 | tf_op jit(solution)/shard_map/reduce_scatter | solution.py:91
  183.9 0.7 copy-start.12
  183.9 154.2 %copy-start.4 = (bf16[128,2048]{1,0:T(8,128)(2,1)S(1)}, bf16[128,2048]{1,0:T(8,128)(2,1)}, u32[]{:S(2)}) copy-start(bf16[128,2048]{1,0:T(8,128)(2,1)} %param.28) | copy-start | bytes 1572868
  183.9 244.2 %reduce-scatter.6.cloned.1.call-start = ((), (), s32[]{:S(2)}) async-start(), calls=%async_computation.8 | async-start | bytes 8912896 | tf_op jit(solution)/shard_map/reduce_scatter | solution.py:100
  343.6 84.5 %copy-start.3 = (bf16[64,2048]{1,0:T(8,128)(2,1)S(1)}, bf16[64,2048]{1,0:T(8,128)(2,1)}, u32[]{:S(2)}) copy-start(bf16[64,2048]{1,0:T(8,128)(2,1)} %param.21) | copy-start | bytes 786436
  343.6 85.8 %copy-start.7 = (f32[2048]{0:T(1024)S(1)}, f32[2048]{0:T(1024)}, u32[]{:S(2)}) copy-start(f32[2048]{0:T(1024)} %param.29) | copy-start | bytes 24580
  343.6 88.8 %copy-start.8 = (s32[128]{0:T(128)S(1)}, s32[128]{0:T(128)}, u32[]{:S(2)}) copy-start(s32[128]{0:T(128)} %param.37) | copy-start | bytes 1540
  343.6 173.7 %all-gather.5.cloned.1.call-start = ((), (), s32[]{:S(2)}) async-start(), calls=%async_computation.9 | async-start | bytes 4456448 | tf_op jit(solution)/shard_map/all_gather | solution.py:108
  445.5 9.2 %copy-start.5 = (s32[8192,4]{0,1:T(4,128)S(1)}, s32[8192,4]{0,1:T(4,128)}, u32[]{:S(2)}) copy-start(s32[8192,4]{0,1:T(4,128)} %param.38) | copy-start | bytes 393220
  445.5 71.8 %copy-start.11 = (bf16[2048,352]{0,1:T(8,128)(2,1)S(1)}, bf16[2048,352]{0,1:T(8,128)(2,1)}, u32[]{:S(2)}) copy-start(bf16[2048,352]{0,1:T(8,128)(2,1)} %param.33) | copy-start | bytes 4325380
  445.5 85.8 %all-to-all-start = ((bf16[128,6,2048]{2,1,0:T(8,128)(2,1)}), bf16[128,6,2048]{2,1,0:T(8,128)(2,1)}, u32[]{:S(2)}, u32[]{:S(2)}) async-start(bf16[128,6,2048]{2,1,0:T(8,128)(2,1)} %reshape.205), calls=%async_computation.3 | async-start | bytes 8388608 | tf_op jit(solution)/shard_map/all_to_all | solution.py:156
  454.0 239.7 %reduce-scatter.8.cloned.1.call-start = ((), (), s32[]{:S(2)}) async-start(), calls=%async_computation.10 | async-start | bytes 4456448 | tf_op jit(solution)/shard_map/reduce_scatter | solution.py:112
  610.7 15.3 %copy-start.10 = (f32[64,4]{0,1:T(4,128)S(1)}, f32[64,4]{0,1:T(4,128)}, u32[]{:S(2)}) copy-start(f32[64,4]{0,1:T(4,128)} %param.39) | copy-start | bytes 3076
  610.7 16.0 %copy-start.9 = (bf16[2048]{0:T(1024)(128)(2,1)S(1)}, bf16[2048]{0:T(1024)(128)(2,1)}, u32[]{:S(2)}) copy-start(bf16[2048]{0:T(1024)(128)(2,1)} %param.36) | copy-start | bytes 12292
  610.7 16.0 %copy-start.2 = (bf16[64,2048]{1,0:T(8,128)(2,1)S(1)}, bf16[64,2048]{1,0:T(8,128)(2,1)}, u32[]{:S(2)}) copy-start(bf16[64,2048]{1,0:T(8,128)(2,1)} %multiply_convert_fusion) | copy-start | bytes 786436
  610.8 66.0 %all-to-all-start.1 = ((bf16[128,6,2048]{2,1,0:T(8,128)(2,1)}), bf16[128,6,2048]{2,1,0:T(8,128)(2,1)}, u32[]{:S(2)}, u32[]{:S(2)}) async-start(bf16[128,6,2048]{2,1,0:T(8,128)(2,1)} %reshape.207), calls=%async_computation.4 | async-start | bytes 8388608 | tf_op jit(solution)/shard_map/all_to_all | solution.py:175
  683.1 12.8 %copy-start.1 = (bf16[352,2048]{1,0:T(8,128)(2,1)S(1)}, bf16[352,2048]{1,0:T(8,128)(2,1)}, u32[]{:S(2)}) copy-start(bf16[352,2048]{1,0:T(8,128)(2,1)} %param.35) | copy-start | bytes 4325380
Sparse Core Ops, SparseCore 0:
  9.5 54.1 all-gather.2
  80.9 80.5 all-reduce.3
  170.3 80.1 all-reduce.5
  253.8 84.2 reduce-scatter.3
  343.7 84.3 reduce-scatter.5
  431.4 85.8 all-gather.4
  531.4 78.5 reduce-scatter.7
where the time goes:
time: 713 us; the launch traced here: 703 us
  waiting for transfers between devices  463 us (65%)
  matrix products  100 us (14%)
  local copies, waits for them, and re-layouts  63.1 us (9%)
  starting transfers between devices  34.9 us (5%)
  other arithmetic  26.4 us (4%)
  between operations  15.3 us (2%)
    reduce_scatter x1, waiting for transfers between devices, shards(): lax.psum_scatter(numerators, 'exp', scatter_dimension=1, tiled=True)  86.1 us
    pmax x1, waiting for transfers between devices, shards(): top = lax.pmax(jnp.max(scores, axis=2), 'exp')  79.2 us
    reduce_scatter x1, waiting for transfers between devices, shards(): lax.psum_scatter(jnp.dot(attention, out_proj, preferred_element_type=jnp....  73.5 us
    unnamed x8, waiting for transfers between devices  66.2 us
    all_gather x1, waiting for transfers between devices, shards(): piece = lax.all_gather(normed, 'exp', axis=0, tiled=True)  55.2 us
    all_gather x1, waiting for transfers between devices, shards(): whole_queries = lax.all_gather(queries, 'exp', axis=0, tiled=True)  52.9 us
    all_to_all x1, waiting for transfers between devices, shards(): lax.all_to_all(answered, ('req', 'exp'), split_axis=0, concat_axis=0, til...  49.8 us
    dot_general x5, matrix products, expert_block(): jnp.dot(hidden, down_w, preferred_element_type=jnp.float32)  36.6 us
  transfers between devices with their start and end apart: 9, of which 7 were waited for; matrix products, arithmetic and copies ran while one was open for 22% of the time, Pallas kernels for 0%

commit v1 on v0

--- a/solution.py
+++ b/solution.py
@@ -1,5 +1,3 @@
-import math
-
 import jax
 import jax.numpy as jnp
 from jax import lax
@@ -20,6 +18,12 @@
 def rms_normed(stream, norm_gain):
     scale_row = lax.rsqrt(jnp.mean(stream * stream, axis=1, keepdims=True) + 1e-06)
     return (stream * scale_row * norm_gain[None, :]).astype(jnp.bfloat16)
+
+
+def gather_exp(piece, count):
+    spread = jnp.broadcast_to(piece[None], (count,) + piece.shape)
+    got = lax.all_to_all(spread, "exp", 0, 0, tiled=True)
+    return got.reshape((count * piece.shape[0],) + piece.shape[1:])
 
 
 def shards(
@@ -56,7 +60,10 @@
     req_slots = page_table.shape[0]
     max_pages = page_table.shape[1]
     capacity = 3 * tok_rows * TOPK // slot_count
-    whole_queries = lax.all_gather(queries, "exp", axis=0, tiled=True)
+
+    whole_proj = lax.all_gather(out_proj, "exp", axis=0, tiled=True)
+
+    whole_queries = gather_exp(queries, exp_count)
     page_ids = exp_index * pages_here + jnp.arange(pages_here, dtype=jnp.int32)
     hits = (page_table[None, :, :] == page_ids[:, None, None]).astype(jnp.int32)
     page_request = jnp.sum(
@@ -78,48 +85,54 @@
         "rhd,khd->hrk", query_heads, key_heads, preferred_element_type=jnp.float32
     ) * HEAD_DIM ** (-0.5)
     scores = jnp.where(visible[None], scores, -1e30)
-    top = lax.pmax(jnp.max(scores, axis=2), "exp")
-    weights = jnp.where(visible[None], jnp.exp(scores - top[:, :, None]), 0.0)
-    denominators = jnp.transpose(jnp.sum(weights, axis=2))
+    local_top = jnp.max(scores, axis=2)
+    weights = jnp.where(visible[None], jnp.exp(scores - local_top[:, :, None]), 0.0)
+    local_den = jnp.sum(weights, axis=2)
     numerators = jnp.einsum(
         "hrk,khd->rhd",
         weights.astype(jnp.bfloat16),
         value_heads,
         preferred_element_type=jnp.float32,
-    ).reshape(group_rows, model_width)
-    num_cols, den_cols = (
-        lax.psum_scatter(numerators, "exp", scatter_dimension=1, tiled=True),
-        lax.psum_scatter(denominators, "exp", scatter_dimension=1, tiled=True),
+    ).reshape(exp_count, tok_rows, model_width)
+    stats = jnp.concatenate(
+        [jnp.transpose(local_top), jnp.transpose(local_den)], axis=1
+    ).reshape(exp_count, tok_rows, 2 * HEADS)
+    got_num = lax.all_to_all(numerators.astype(jnp.bfloat16), "exp", 0, 0, tiled=True)
+    got_stats = lax.all_to_all(stats, "exp", 0, 0, tiled=True)
+    part_top = got_stats[:, :, :HEADS]
+    part_den = got_stats[:, :, HEADS:]
+    top = jnp.max(part_top, axis=0)
+    shift = jnp.exp(part_top - top[None])
+    denominators = jnp.sum(shift * part_den, axis=0)
+    combined = jnp.sum(
+        got_num.astype(jnp.float32).reshape(exp_count, tok_rows, HEADS, HEAD_DIM)
+        * shift[:, :, :, None],
+        axis=0,
     )
-    local_heads = den_cols.shape[1]
     attention = (
-        (num_cols.reshape(group_rows, local_heads, HEAD_DIM) / den_cols[:, :, None])
-        .reshape(group_rows, local_heads * HEAD_DIM)
-        .astype(jnp.bfloat16)
+        (combined / denominators[:, :, None]).reshape(tok_rows, model_width).astype(jnp.bfloat16)
     )
-    mixed = lax.psum_scatter(
-        jnp.dot(attention, out_proj, preferred_element_type=jnp.float32),
-        "exp",
-        scatter_dimension=0,
-        tiled=True,
-    )
+    mixed = jnp.dot(attention, whole_proj, preferred_element_type=jnp.float32)
     stream = resid.astype(jnp.float32) + mixed
     normed = rms_normed(stream, norm_gain)
-    piece = lax.all_gather(normed, "exp", axis=0, tiled=True)
+
+    piece = gather_exp(normed, exp_count)
     gate = jnp.dot(piece, shared_gate, preferred_element_type=jnp.float32)
     upper = jnp.dot(piece, shared_up, preferred_element_type=jnp.float32)
     shared_hidden = (jax.nn.silu(gate) * upper).astype(jnp.bfloat16)
-    shared_out = lax.psum_scatter(
-        jnp.dot(shared_hidden, shared_down, preferred_element_type=jnp.float32).astype(
-            jnp.bfloat16
-        ),
-        "exp",
-        scatter_dimension=0,
-        tiled=True,
-    ).astype(jnp.float32)
+    shared_part = jnp.dot(
+        shared_hidden, shared_down, preferred_element_type=jnp.float32
+    ).astype(jnp.bfloat16)
+    shared_out = jnp.sum(
+        lax.all_to_all(
+            shared_part.reshape(exp_count, tok_rows, model_width), "exp", 0, 0, tiled=True
+        ).astype(jnp.float32),
+        axis=0,
+    )
     shared_scale = jax.nn.sigmoid(
         jnp.dot(normed, shared_scalar, preferred_element_type=jnp.float32)
     )
+
     slot_ids = jnp.arange(slot_count, dtype=jnp.int32)
     same_expert = slot_expert[:, None] == slot_expert[None, :]
     copy_rank = jnp.sum(
@@ -129,13 +142,7 @@
         -1
     )
     holds = own_routes[:, None] == slot_expert[None, :]
-    copy_total = jnp.sum(holds.astype(jnp.int32), axis=1)
-    own_mark = slot_ids == own_slot
-    own_expert = jnp.sum(jnp.where(own_mark, slot_expert, 0))
-    own_rank = jnp.sum(jnp.where(own_mark, copy_rank, 0))
-    wanted = jnp.zeros_like(copy_total)
-    taken = jnp.broadcast_to(own_rank == 0, (slot_count,))
-    chosen = holds & (copy_rank[None, :] == wanted[:, None])
+    chosen = holds & (copy_rank[None, :] == 0)
     target = jnp.sum(jnp.where(chosen, slot_ids[None, :], 0), axis=1)
     onehot = chosen.astype(jnp.int32)
     position = jnp.sum(jnp.cumsum(onehot, axis=0) * onehot, axis=1) - 1
@@ -147,31 +154,10 @@
         .set(entry_rows)
     )
     outgoing = outgoing.reshape(slot_count, capacity, model_width)
-    named = (
-        jnp.sum((route_expert == own_expert).astype(jnp.int32), axis=1)
-        .reshape(slot_count, tok_rows)
-        .sum(axis=1)
-    )
-    arrived = jnp.where(taken, named, 0)
     incoming = lax.all_to_all(outgoing, ("req", "exp"), split_axis=0, concat_axis=0, tiled=True)
-    filled = (jnp.arange(capacity, dtype=jnp.int32)[None, :] < arrived[:, None]).reshape(-1)
-    packed_order = jnp.argsort(1 - filled.astype(jnp.int32), stable=True)
-    packed = incoming.reshape(-1, model_width)[packed_order]
-    live = jnp.sum(filled.astype(jnp.int32))
-    tile = math.gcd(128, slot_count * capacity)
-
-    def tile_step(step, results):
-        rows = lax.dynamic_slice_in_dim(packed, step * tile, tile, 0)
-        answer = expert_block(rows, expert_gate[0], expert_up[0], expert_down[0])
-        return lax.dynamic_update_slice_in_dim(results, answer, step * tile, 0)
-
-    results = lax.fori_loop(0, (live + tile - 1) // tile, tile_step, jnp.zeros_like(packed))
-    answered = (
-        jnp.zeros_like(results)
-        .at[packed_order]
-        .set(results)
-        .reshape(slot_count, capacity, model_width)
-    )
+    answered = expert_block(
+        incoming.reshape(-1, model_width), expert_gate[0], expert_up[0], expert_down[0]
+    ).reshape(slot_count, capacity, model_width)
     returned = lax.all_to_all(
         answered, ("req", "exp"), split_axis=0, concat_axis=0, tiled=True
     ).reshape(-1, model_width)

time: 713 us -> 499 us (0.70)
  waiting for transfers between devices: 463 us -> 214 us
  blocking collectives: 0 us -> 58.8 us
  matrix products: 100 us -> 64 us
  local copies, waits for them, and re-layouts: 63.1 us -> 82.1 us
    all_to_all x1 -> x5, waiting for transfers between devices: 0.01 us -> 177 us  [the longest x2 90.6 us: gather_exp(): got = lax.all_to_all(spread, 'exp', 0, 0, tiled=True)]
    reduce_scatter x3 -> x0, waiting for transfers between devices: 160 us -> none  [the longest x1 86.1 us: shards(): lax.psum_scatter(numerators, 'exp', scatter_dimension=1, tiled=True)]
    all_gather x2 -> x1, waiting for transfers between devices: 108 us -> 0.02 us  [shards(): whole_proj = lax.all_gather(out_proj, 'exp', axis=0, tiled=True)]
    pmax x1 -> x0, waiting for transfers between devices: 79.2 us -> none  [shards(): top = lax.pmax(jnp.max(scores, axis=2), 'exp')]
    unnamed x8 -> x1, waiting for transfers between devices: 66.2 us -> 0.71 us
    all_to_all x0 -> x1, blocking collectives: none -> 58.8 us  [shards(): lax.all_to_all(outgoing, ('req', 'exp'), split_axis=0, concat_axis=0, til...]
    all_to_all x1 -> x5, starting transfers between devices: 8.44 us -> 29.7 us  [the longest x2 13 us: gather_exp(): got = lax.all_to_all(spread, 'exp', 0, 0, tiled=True)]
    dot_general x5 -> x1, matrix products: 36.6 us -> 16.9 us  [expert_block(): jnp.dot(hidden, down_w, preferred_element_type=jnp.float32)]
  transfers between devices with their start and end apart: 9 -> 7, of which waited for: 7 -> 5; matrix products, arithmetic and copies ran while one was open for 22% -> 29% of each run, Pallas kernels for 0% -> 0%
where the time goes in v1:
time: 499 us; the launch traced here: 492 us
  waiting for transfers between devices  214 us (43%)
  local copies, waits for them, and re-layouts  82.1 us (16%)
  matrix products  64 us (13%)
  blocking collectives  58.8 us (12%)
  starting transfers between devices  35.6 us (7%)
  other arithmetic  23.7 us (5%)
  between operations  14 us (3%)
    all_to_all x2, waiting for transfers between devices, gather_exp(): got = lax.all_to_all(spread, 'exp', 0, 0, tiled=True)  90.6 us
    all_to_all x1, blocking collectives, shards(): lax.all_to_all(outgoing, ('req', 'exp'), split_axis=0, concat_axis=0, til...  58.8 us
    all_to_all x1, waiting for transfers between devices, shards(): lax.all_to_all(shared_part.reshape(exp_count, tok_rows, model_width), 'ex...  45.5 us
    all_to_all x1, waiting for transfers between devices, shards(): lax.all_to_all(numerators.astype(jnp.bfloat16), 'exp', 0, 0, tiled=True)  40.9 us
    all_to_all x1, waiting for transfers between devices, shards(): lax.all_to_all(answered, ('req', 'exp'), split_axis=0, concat_axis=0, til...  36.4 us
    dot_general x1, matrix products, expert_block(): jnp.dot(hidden, down_w, preferred_element_type=jnp.float32)  16.9 us
    mul x2, local copies, waits for them, and re-layouts, shards(): got_num.astype(jnp.float32).reshape(exp_count, tok_rows, HEADS, HEAD_DIM)  13.9 us
    all_to_all x2, starting transfers between devices, gather_exp(): got = lax.all_to_all(spread, 'exp', 0, 0, tiled=True)  13 us
  transfers between devices with their start and end apart: 7, of which 5 were waited for; matrix products, arithmetic and copies ran while one was open for 29% of the time, Pallas kernels for 0%

profile of v1, /device:TPU:0, one launch (start us, length us, event | category | flops | bytes accessed | tf_op | source)
XLA Modules:
  0.0 492.3 jit_solution(2614587570008969038)
XLA Ops:
  6.5 0.7 all-gather.2.cloned.1.call-update
  7.3 3.4 broadcast_in_dim.38
  10.7 8.1 %all-to-all-start = ((bf16[16,64,2048]{2,1,0:T(8,128)(2,1)}), bf16[16,64,2048]{2,1,0:T(8,128)(2,1)}, u32[]{:S(2)}, u32[]{:S(2)}) async-start(bf16[16,64,2048]{2,1,0:T(8,128)(2,1)} %broadcast_in_dim.38), calls=%async_computation | async-start | bytes 8388608 | tf_op jit(solution)/shard_map/all_to_all | solution.py:25
  18.9 1.3 copy.80
  20.2 1.3 copy.81
  21.5 0.2 fusion.46
  21.8 0.3 compare_and_fusion
  22.1 66.3 %all-to-all-done = bf16[16,64,2048]{2,1,0:T(8,128)(2,1)} async-done(((bf16[16,64,2048]{2,1,0:T(8,128)(2,1)}), bf16[16,64,2048]{2,1,0:T(8,128)(2,1)}, u32[]{:S(2)}, u32[]{:S(2)}) %all-to-all-start) | async-done | bytes 4194336 | tf_op jit(solution)/shard_map/all_to_all | solution.py:25
  88.4 3.7 copy.79
  92.1 8.3 %fusion = (f32[16,1024]{1,0:T(8,128)S(1)}, f32[16,1024,256]{1,2,0:T(8,128)}) fusion(pred[1024,256]{0,1:T(8,128)(4,1)S(1)} %compare_and_fusion, bf16[256,16,128]{2,1,0:T(8,128)(2,1)S(1)} %bitcast.92, bf16[1024,16,128]{2,1,0:T(8,128)(2,1)S(1)} %bitcast.86), kind=kOutput, calls=%fused_computation.4 | convolution fusion | flops 1086308352 | bytes 22347776 | tf_op jit(solution)/shard_map/rhd,khd->hrk/dot_general | solution.py:84
  100.4 8.3 %fusion.1 = f32[16,1024]{1,0:T(8,128)S(1)} fusion(f32[16,1024,256]{1,2,0:T(8,128)} %get-tuple-element.12, f32[16,1024]{1,0:T(8,128)S(1)} %get-tuple-element.11, pred[1024,256]{0,1:T(8,128)(4,1)S(1)} %compare_and_fusion), kind=kLoop, calls=%fused_computation.5 | loop fusion | flops 20955136 | bytes 17170432 | tf_op jit(solution)/shard_map/reduce_sum | solution.py:90
  108.8 0.1 reshape.201
  109.0 0.8 reshape.231
  109.8 3.8 all-to-all-start.2
  113.6 9.4 %convert_bitcast_fusion = bf16[1024,16,128]{2,0,1:T(8,128)(2,1)S(1)} fusion(f32[16,1024,256]{1,2,0:T(8,128)} %get-tuple-element.12, f32[16,1024]{1,0:T(8,128)S(1)} %get-tuple-element.11, pred[1024,256]{0,1:T(8,128)(4,1)S(1)} %compare_and_fusion, bf16[256,16,128]{2,1,0:T(8,128)(2,1)S(1)} %bitcast.91), kind=kOutput, calls=%fused_computation.24 | convolution fusion | flops 1096810496 | bytes 22347776 | tf_op jit(solution)/shard_map/hrk,khd->rhd/dot_general | solution.py:91
  123.0 4.6 copy.67
  127.7 7.3 %convert_element_type.61 = bf16[16,64,2048]{2,1,0:T(8,128)(2,1)} reshape(bf16[1024,16,128]{2,1,0:T(8,128)(2,1)} %copy.67) | data formatting | bytes 8388608 | tf_op jit(solution)/shard_map/convert_element_type | solution.py:100
  135.0 8.0 %all-to-all-start.1 = ((bf16[16,64,2048]{2,1,0:T(8,128)(2,1)}), bf16[16,64,2048]{2,1,0:T(8,128)(2,1)}, u32[]{:S(2)}, u32[]{:S(2)}) async-start(bf16[16,64,2048]{2,1,0:T(8,128)(2,1)} %convert_element_type.61), calls=%async_computation.1 | async-start | bytes 8388608 | tf_op jit(solution)/shard_map/all_to_all | solution.py:100
  143.0 0.8 constant_dynamic-slice_fusion
  143.7 0.1 copy.72
  143.8 0.1 eq.97
  143.9 0.1 eq.88
  144.0 0.1 copy.74
  144.2 0.2 convert_reduce_fusion.1
  144.3 0.2 fusion.39
  144.7 0.2 select_reduce_fusion
  144.9 0.5 broadcast.173
  145.4 0.9 reduce.1
  146.4 0.1 reshape.232
  146.6 0.2 copy.69
  146.8 4.6 mul.127
  151.4 9.3 %mul.128 = f32[16,64,2048]{2,1,0:T(8,128)} reshape(f32[16,64,16,128]{3,2,1,0:T(8,128)} %mul.127) | data formatting | bytes 16777216 | tf_op jit(solution)/shard_map/mul | solution.py:108
  160.7 40.9 %all-to-all-done.1 = bf16[16,64,2048]{2,1,0:T(8,128)(2,1)} async-done(((bf16[16,64,2048]{2,1,0:T(8,128)(2,1)}), bf16[16,64,2048]{2,1,0:T(8,128)(2,1)}, u32[]{:S(2)}, u32[]{:S(2)}) %all-to-all-start.1) | async-done | bytes 4194336 | tf_op jit(solution)/shard_map/all_to_all | solution.py:100
  201.6 5.9 %multiply_reduce_fusion = f32[64,2048]{1,0:T(8,128)S(1)} fusion(f32[16,64,2048]{2,1,0:T(8,128)} %mul.128, bf16[16,64,2048]{2,1,0:T(8,128)(2,1)} %all-to-all-done.1), kind=kLoop, calls=%fused_computation.9 | loop fusion | flops 6160384 | bytes 13107200 | tf_op jit(solution)/shard_map/reduce_sum | solution.py:107
  207.6 0.2 div.28
  207.8 5.2 %multiply_reduce_fusion.2 = (f32[64]{0:T(128)S(1)}, f32[64,2048]{1,0:T(8,128)S(1)}) fusion(bf16[2048,2048]{1,0:T(8,128)(2,1)} %all-gather.2.cloned.1.call-done, f32[64,2048]{1,0:T(8,128)S(1)} %multiply_reduce_fusion, f32[8,8,16,128]{3,2,1,0:T(8,128)S(1)} %bitcast.84, bf16[64,2048]{1,0:T(8,128)(2,1)S(1)} %copy-done.8), kind=kOutput, calls=%fused_computation.46 | convolution fusion | flops 537657280 | bytes 10223872 | tf_op jit(solution)/shard_map/dot_general | solution.py:115
  213.0 0.8 copy-done.1
  213.8 0.1 multiply_convert_fusion.1
  213.9 0.5 broadcast_in_dim.49
  214.4 1.1 reshape.223
  215.5 5.0 %scatter_custom_fusion = bf16[768,2048]{1,0:T(8,128)(2,1)} fusion(s32[256]{0:T(256)S(1)} %bitcast.99, bf16[256,2048]{1,0:T(8,128)(2,1)} %reshape.223, bf16[]{:T(256)} %constant.18.clone.1), kind=kCustom, calls=%fused_computation.29 | custom fusion | bytes 3146240 | tf_op jit(solution)/shard_map/scatter | solution.py:154
  220.5 6.3 %reshape.206 = bf16[128,6,2048]{2,1,0:T(8,128)(2,1)} reshape(bf16[768,2048]{1,0:T(8,128)(2,1)} %scatter_custom_fusion) | data formatting | bytes 6291456 | tf_op jit(solution)/shard_map/reshape | solution.py:156
  226.8 58.8 %all_to_all.35 = bf16[128,6,2048]{2,1,0:T(8,128)(2,1)} all-to-all(bf16[128,6,2048]{2,1,0:T(8,128)(2,1)} %reshape.206), channel_id=1, replica_groups=mesh['req'=8,'exp'=16] {'req','exp'}, dimensions={0} | all-to-all | bytes 6291456 | tf_op jit(solution)/shard_map/all_to_all | solution.py:157
  285.5 2.5 broadcast_in_dim.41
  288.0 4.8 all-to-all-start.3
  292.8 6.3 %reshape.207 = bf16[768,2048]{1,0:T(8,128)(2,1)} reshape(bf16[128,6,2048]{2,1,0:T(8,128)(2,1)} %all_to_all.35) | data formatting | bytes 6291456 | tf_op jit(solution)/shard_map/reshape | solution.py:159
  299.2 9.7 %fusion.12 = f32[768,1408]{1,0:T(8,128)} fusion(bf16[768,2048]{1,0:T(8,128)(2,1)} %reshape.207, bf16[1,2048,1408]{2,1,0:T(8,128)(2,1)} %param.29), kind=kOutput, calls=%fused_computation.17 | convolution fusion | flops 4429185024 | bytes 13238272 | tf_op jit(solution)/shard_map/dot_general | solution.py:13
  308.8 16.9 %fusion.20 = bf16[768,2048]{1,0:T(8,128)(2,1)} fusion(bf16[1,1408,2048]{2,1,0:T(8,128)(2,1)} %param.30, f32[768,1408]{1,0:T(8,128)} %fusion.12, bf16[768,2048]{1,0:T(8,128)(2,1)} %reshape.207, bf16[1,2048,1408]{2,1,0:T(8,128)(2,1)} %param.28), kind=kOutput, calls=%fused_computation.26 | convolution fusion | flops 8866430976 | bytes 22151168 | tf_op jit(solution)/shard_map/dot_general | solution.py:15
  325.8 6.3 %reshape.208 = bf16[128,6,2048]{2,1,0:T(8,128)(2,1)} reshape(bf16[768,2048]{1,0:T(8,128)(2,1)} %fusion.20) | data formatting | bytes 6291456 | tf_op jit(solution)/shard_map/reshape | solution.py:160
  332.0 24.3 %all-to-all-done.3 = bf16[16,64,2048]{2,1,0:T(8,128)(2,1)} async-done(((bf16[16,64,2048]{2,1,0:T(8,128)(2,1)}), bf16[16,64,2048]{2,1,0:T(8,128)(2,1)}, u32[]{:S(2)}, u32[]{:S(2)}) %all-to-all-start.3) | async-done | bytes 4194336 | tf_op jit(solution)/shard_map/all_to_all | solution.py:25
  356.3 5.9 %all-to-all-start.6 = ((bf16[128,6,2048]{2,1,0:T(8,128)(2,1)}), bf16[128,6,2048]{2,1,0:T(8,128)(2,1)}, u32[]{:S(2)}, u32[]{:S(2)}) async-start(bf16[128,6,2048]{2,1,0:T(8,128)(2,1)} %reshape.208), calls=%async_computation.6 | async-start | bytes 8388608 | tf_op jit(solution)/shard_map/all_to_all | solution.py:161
  362.2 5.4 %fusion.53 = f32[1024,352]{0,1:T(8,128)} fusion(bf16[1024,2048]{1,0:T(8,128)(2,1)} %bitcast.6, bf16[2048,352]{0,1:T(8,128)(2,1)} %param.31), kind=kOutput, calls=%fused_computation.86 | convolution fusion | flops 1476395008 | bytes 7077888 | tf_op jit(solution)/shard_map/dot_general | solution.py:120
  367.6 8.9 %convolution_convert_fusion = bf16[1024,2048]{1,0:T(8,128)(2,1)} fusion(bf16[352,2048]{1,0:T(8,128)(2,1)S(1)} %copy-done, bf16[1024,2048]{1,0:T(8,128)(2,1)} %bitcast.6, bf16[2048,352]{0,1:T(8,128)(2,1)} %param.32, f32[1024,352]{0,1:T(8,128)} %fusion.53), kind=kOutput, calls=%fused_computation.25 | convolution fusion | flops 2957049856 | bytes 12713984 | tf_op jit(solution)/shard_map/dot_general | solution.py:123
  376.6 36.4 %all-to-all-done.6 = bf16[128,6,2048]{2,1,0:T(8,128)(2,1)} async-done(((bf16[128,6,2048]{2,1,0:T(8,128)(2,1)}), bf16[128,6,2048]{2,1,0:T(8,128)(2,1)}, u32[]{:S(2)}, u32[]{:S(2)}) %all-to-all-start.6) | async-done | bytes 3145760 | tf_op jit(solution)/shard_map/all_to_all | solution.py:161
  412.9 5.0 %all-to-all-start.4 = ((bf16[16,64,2048]{2,1,0:T(8,128)(2,1)}), bf16[16,64,2048]{2,1,0:T(8,128)(2,1)}, u32[]{:S(2)}, u32[]{:S(2)}) async-start(bf16[16,64,2048]{2,1,0:T(8,128)(2,1)} %bitcast.85), calls=%async_computation.4 | async-start | bytes 8388608 | tf_op jit(solution)/shard_map/all_to_all | solution.py:127
  418.0 0.7 copy.76
  418.7 0.2 fusion.31
  418.9 6.4 %reshape.209 = bf16[768,2048]{1,0:T(8,128)(2,1)} reshape(bf16[128,6,2048]{2,1,0:T(8,128)(2,1)} %all-to-all-done.6) | data formatting | bytes 6291456 | tf_op jit(solution)/shard_map/reshape | solution.py:163
  425.2 5.7 %gather_fusion = bf16[256,2048]{1,0:T(8,128)(2,1)} fusion(bf16[768,2048]{1,0:T(8,128)(2,1)} %reshape.209, s32[1024]{0:T(1024)S(1)} %pad_clamp_fusion), kind=kCustom, calls=%fused_computation | custom fusion | bytes 2098176 | tf_op jit(solution)/shard_map/gather | solution.py:164
  430.9 1.7 reshape.210
  432.7 3.2 multiply_reduce_fusion.1
  435.8 45.5 %all-to-all-done.4 = bf16[16,64,2048]{2,1,0:T(8,128)(2,1)} async-done(((bf16[16,64,2048]{2,1,0:T(8,128)(2,1)}), bf16[16,64,2048]{2,1,0:T(8,128)(2,1)}, u32[]{:S(2)}, u32[]{:S(2)}) %all-to-all-start.4) | async-done | bytes 4194336 | tf_op jit(solution)/shard_map/all_to_all | solution.py:127
  481.4 3.0 convert_reduce_fusion
  484.4 0.8 add_convert_fusion
  (54 shorter events, 0.5 us)
Async XLA Ops:
  6.5 361.1 %copy-start = (bf16[352,2048]{1,0:T(8,128)(2,1)S(1)}, bf16[352,2048]{1,0:T(8,128)(2,1)}, u32[]{:S(2)}) copy-start(bf16[352,2048]{1,0:T(8,128)(2,1)} %param.33) | copy-start | bytes 4325380
  6.5 201.1 %all-gather.2.cloned.1.call-start = ((), (), s32[]{:S(2)}) async-start(), calls=%async_computation.7 | async-start | bytes 8912896 | tf_op jit(solution)/shard_map/all_gather | solution.py:64
  10.7 8.2 %copy-start.4 = (bf16[2,128,2048]{2,1,0:T(8,128)(2,1)S(1)}, bf16[2,128,2048]{2,1,0:T(8,128)(2,1)}, u32[]{:S(2)}) copy-start(bf16[2,128,2048]{2,1,0:T(8,128)(2,1)} %param.21) | copy-start | bytes 3145732
  10.7 9.5 %copy-start.5 = (bf16[2,128,2048]{2,1,0:T(8,128)(2,1)S(1)}, bf16[2,128,2048]{2,1,0:T(8,128)(2,1)}, u32[]{:S(2)}) copy-start(bf16[2,128,2048]{2,1,0:T(8,128)(2,1)} %param.22) | copy-start | bytes 3145732
  10.7 77.7 %all-to-all-start = ((bf16[16,64,2048]{2,1,0:T(8,128)(2,1)}), bf16[16,64,2048]{2,1,0:T(8,128)(2,1)}, u32[]{:S(2)}, u32[]{:S(2)}) async-start(bf16[16,64,2048]{2,1,0:T(8,128)(2,1)} %broadcast_in_dim.38), calls=%async_computation | async-start | bytes 8388608 | tf_op jit(solution)/shard_map/all_to_all | solution.py:25
  18.9 2.7 copy-start.15
  18.9 3.0 copy-start.10
  18.9 2.9 copy-start.11
  88.4 3.7 copy-start.7
  100.4 13.2 %copy-start.6 = (bf16[32,8,16,128]{3,2,1,0:T(8,128)(2,1)S(1)}, bf16[32,8,16,128]{3,2,1,0:T(8,128)(2,1)}, u32[]{:S(2)}) copy-start(bf16[32,8,16,128]{3,2,1,0:T(8,128)(2,1)} %copy.81) | copy-start | bytes 3145732
  109.8 25.2 %all-to-all-start.2 = ((f32[16,1,2048]{2,1,0:T(1,128)}), f32[16,1,2048]{2,1,0:T(1,128)S(1)}, u32[]{:S(2)}, u32[]{:S(2)}) async-start(f32[16,1,2048]{2,1,0:T(1,128)} %reshape.231), calls=%async_computation.2 | async-start | bytes 262144 | tf_op jit(solution)/shard_map/all_to_all | solution.py:101
  135.0 9.2 %copy-start.13 = (s32[128]{0:T(128)S(1)}, s32[128]{0:T(128)}, u32[]{:S(2)}) copy-start(s32[128]{0:T(128)} %param.35) | copy-start | bytes 1540
  135.0 66.6 %all-to-all-start.1 = ((bf16[16,64,2048]{2,1,0:T(8,128)(2,1)}), bf16[16,64,2048]{2,1,0:T(8,128)(2,1)}, u32[]{:S(2)}, u32[]{:S(2)}) async-start(bf16[16,64,2048]{2,1,0:T(8,128)(2,1)} %convert_element_type.61), calls=%async_computation.1 | async-start | bytes 8388608 | tf_op jit(solution)/shard_map/all_to_all | solution.py:100
  160.7 47.1 %copy-start.8 = (bf16[64,2048]{1,0:T(8,128)(2,1)S(1)}, bf16[64,2048]{1,0:T(8,128)(2,1)}, u32[]{:S(2)}) copy-start(bf16[64,2048]{1,0:T(8,128)(2,1)} %param.19) | copy-start | bytes 786436
  207.8 6.0 %copy-start.9 = (f32[2048]{0:T(1024)S(1)}, f32[2048]{0:T(1024)}, u32[]{:S(2)}) copy-start(f32[2048]{0:T(1024)} %param.27) | copy-start | bytes 24580
  213.0 0.8 copy-start.1
  288.0 68.3 %all-to-all-start.3 = ((bf16[16,64,2048]{2,1,0:T(8,128)(2,1)}), bf16[16,64,2048]{2,1,0:T(8,128)(2,1)}, u32[]{:S(2)}, u32[]{:S(2)}) async-start(bf16[16,64,2048]{2,1,0:T(8,128)(2,1)} %broadcast_in_dim.41), calls=%async_computation.3 | async-start | bytes 8388608 | tf_op jit(solution)/shard_map/all_to_all | solution.py:25
  356.3 56.6 %all-to-all-start.6 = ((bf16[128,6,2048]{2,1,0:T(8,128)(2,1)}), bf16[128,6,2048]{2,1,0:T(8,128)(2,1)}, u32[]{:S(2)}, u32[]{:S(2)}) async-start(bf16[128,6,2048]{2,1,0:T(8,128)(2,1)} %reshape.208), calls=%async_computation.6 | async-start | bytes 8388608 | tf_op jit(solution)/shard_map/all_to_all | solution.py:161
  412.9 5.0 %copy-start.12 = (bf16[2048]{0:T(1024)(128)(2,1)S(1)}, bf16[2048]{0:T(1024)(128)(2,1)}, u32[]{:S(2)}) copy-start(bf16[2048]{0:T(1024)(128)(2,1)} %param.34) | copy-start | bytes 12292
  412.9 5.0 %copy-start.14 = (f32[64,4]{0,1:T(4,128)S(1)}, f32[64,4]{0,1:T(4,128)}, u32[]{:S(2)}) copy-start(f32[64,4]{0,1:T(4,128)} %param.37) | copy-start | bytes 3076
  412.9 68.4 %all-to-all-start.4 = ((bf16[16,64,2048]{2,1,0:T(8,128)(2,1)}), bf16[16,64,2048]{2,1,0:T(8,128)(2,1)}, u32[]{:S(2)}, u32[]{:S(2)}) async-start(bf16[16,64,2048]{2,1,0:T(8,128)(2,1)} %bitcast.85), calls=%async_computation.4 | async-start | bytes 8388608 | tf_op jit(solution)/shard_map/all_to_all | solution.py:127
  435.8 48.5 %copy-start.2 = (f32[64,2048]{1,0:T(8,128)S(1)}, f32[64,2048]{1,0:T(8,128)}, u32[]{:S(2)}) copy-start(f32[64,2048]{1,0:T(8,128)} %copy-done.1) | copy-start | bytes 1572868
  435.8 48.5 %copy-start.3 = (f32[64,2048]{1,0:T(8,128)S(1)}, f32[64,2048]{1,0:T(8,128)}, u32[]{:S(2)}) copy-start(f32[64,2048]{1,0:T(8,128)} %multiply_reduce_fusion.1) | copy-start | bytes 1572868
Sparse Core Ops, SparseCore 0:
  9.5 114.3 all-gather.1

commit v2 on v1

--- a/solution.py
+++ b/solution.py
@@ -61,10 +61,18 @@
     max_pages = page_table.shape[1]
     capacity = 3 * tok_rows * TOPK // slot_count
 
-    whole_proj = lax.all_gather(out_proj, "exp", axis=0, tiled=True)
-
-    whole_queries = gather_exp(queries, exp_count)
-    page_ids = exp_index * pages_here + jnp.arange(pages_here, dtype=jnp.int32)
+    query_cols = lax.all_to_all(
+        queries.reshape(tok_rows, HEADS, HEAD_DIM).transpose(1, 0, 2), "exp", 0, 0, tiled=True
+    ).reshape(group_rows, HEAD_DIM)
+    key_count = pages_here * page_len
+    group_keys = exp_count * key_count
+    key_cols = lax.all_to_all(
+        cache_key.reshape(key_count, HEADS, HEAD_DIM).transpose(1, 0, 2), "exp", 0, 0, tiled=True
+    ).reshape(group_keys, HEAD_DIM)
+    value_cols = lax.all_to_all(
+        cache_value.reshape(key_count, HEADS, HEAD_DIM).transpose(1, 0, 2), "exp", 0, 0, tiled=True
+    ).reshape(group_keys, HEAD_DIM)
+    page_ids = jnp.arange(exp_count * pages_here, dtype=jnp.int32)
     hits = (page_table[None, :, :] == page_ids[:, None, None]).astype(jnp.int32)
     page_request = jnp.sum(
         hits * jnp.arange(req_slots, dtype=jnp.int32)[None, :, None], axis=(1, 2)
@@ -77,42 +85,25 @@
     visible = (row_request[:, None] == key_request[None, :]) & (
         key_position[None, :] <= row_position[:, None]
     )
-    key_count = pages_here * page_len
-    query_heads = whole_queries.reshape(group_rows, HEADS, HEAD_DIM)
-    key_heads = cache_key.reshape(key_count, HEADS, HEAD_DIM)
-    value_heads = cache_value.reshape(key_count, HEADS, HEAD_DIM)
-    scores = jnp.einsum(
-        "rhd,khd->hrk", query_heads, key_heads, preferred_element_type=jnp.float32
+    scores = jnp.dot(
+        query_cols, key_cols.T, preferred_element_type=jnp.float32
     ) * HEAD_DIM ** (-0.5)
-    scores = jnp.where(visible[None], scores, -1e30)
-    local_top = jnp.max(scores, axis=2)
-    weights = jnp.where(visible[None], jnp.exp(scores - local_top[:, :, None]), 0.0)
-    local_den = jnp.sum(weights, axis=2)
-    numerators = jnp.einsum(
-        "hrk,khd->rhd",
-        weights.astype(jnp.bfloat16),
-        value_heads,
-        preferred_element_type=jnp.float32,
-    ).reshape(exp_count, tok_rows, model_width)
-    stats = jnp.concatenate(
-        [jnp.transpose(local_top), jnp.transpose(local_den)], axis=1
-    ).reshape(exp_count, tok_rows, 2 * HEADS)
-    got_num = lax.all_to_all(numerators.astype(jnp.bfloat16), "exp", 0, 0, tiled=True)
-    got_stats = lax.all_to_all(stats, "exp", 0, 0, tiled=True)
-    part_top = got_stats[:, :, :HEADS]
-    part_den = got_stats[:, :, HEADS:]
-    top = jnp.max(part_top, axis=0)
-    shift = jnp.exp(part_top - top[None])
-    denominators = jnp.sum(shift * part_den, axis=0)
-    combined = jnp.sum(
-        got_num.astype(jnp.float32).reshape(exp_count, tok_rows, HEADS, HEAD_DIM)
-        * shift[:, :, :, None],
+    scores = jnp.where(visible, scores, -1e30)
+    top = jnp.max(scores, axis=1)
+    weights = jnp.where(visible, jnp.exp(scores - top[:, None]), 0.0)
+    denominators = jnp.sum(weights, axis=1)
+    numerators = jnp.dot(
+        weights.astype(jnp.bfloat16), value_cols, preferred_element_type=jnp.float32
+    )
+    attention = (numerators / denominators[:, None]).astype(jnp.bfloat16)
+    mixed_part = jnp.dot(attention, out_proj, preferred_element_type=jnp.float32)
+    mixed = jnp.sum(
+        lax.all_to_all(
+            mixed_part.astype(jnp.bfloat16).reshape(exp_count, tok_rows, model_width),
+            "exp", 0, 0, tiled=True,
+        ).astype(jnp.float32),
         axis=0,
     )
-    attention = (
-        (combined / denominators[:, :, None]).reshape(tok_rows, model_width).astype(jnp.bfloat16)
-    )
-    mixed = jnp.dot(attention, whole_proj, preferred_element_type=jnp.float32)
     stream = resid.astype(jnp.float32) + mixed
     normed = rms_normed(stream, norm_gain)
 

time: 499 us -> 414 us (0.83); the launches traced: 492 us -> 412 us
  waiting for transfers between devices: 214 us -> 182 us
  local copies, waits for them, and re-layouts: 82.1 us -> 55.7 us
  between operations: 14 us -> 0.4 us
  other arithmetic: 23.7 us -> 17.8 us
    all_to_all x2 -> x1, waiting for transfers between devices: 90.6 us -> 24.1 us  [gather_exp(): got = lax.all_to_all(spread, 'exp', 0, 0, tiled=True)]
    all_to_all x2 -> x4, waiting for transfers between devices: 40.9 us -> 75.1 us  [the longest x1 55.1 us: shards(): lax.all_to_all(mixed_part.astype(jnp.bfloat16).reshape(exp_count, tok_row...]
    mul x2 -> x0, local copies, waits for them, and re-layouts: 13.9 us -> none  [shards(): got_num.astype(jnp.float32).reshape(exp_count, tok_rows, HEADS, HEAD_DIM)]
    convert_element_type x2 -> x0, local copies, waits for them, and re-layouts: 11.9 us -> none  [shards(): numerators.astype(jnp.bfloat16)]
    all_to_all x2 -> x4, starting transfers between devices: 11.8 us -> 22.6 us  [the longest x1 7.96 us: shards(): lax.all_to_all(queries.reshape(tok_rows, HEADS, HEAD_DIM).transpose(1, 0,...]
    all_to_all x2 -> x1, starting transfers between devices: 13 us -> 4.79 us  [gather_exp(): got = lax.all_to_all(spread, 'exp', 0, 0, tiled=True)]
    reduce_sum x3, other arithmetic: 14.3 us -> 9.23 us  [the longest x1 6.06 us: shards(): denominators = jnp.sum(weights, axis=1)]
    dot_general x3 -> x2, matrix products: 22.8 us -> 18.4 us  [the longest x1 12.3 us: shards(): jnp.dot(attention, out_proj, preferred_element_type=jnp.float32)]
  transfers between devices with their start and end apart: 7 -> 7, of which waited for: 5 -> 6; matrix products, arithmetic and copies ran while one was open for 29% -> 22% of each run, Pallas kernels for 0% -> 0%
where the time goes in v2:
time: 414 us; the launch traced here: 412 us
  waiting for transfers between devices  182 us (44%)
  matrix products  59.5 us (14%)
  blocking collectives  58.8 us (14%)
  local copies, waits for them, and re-layouts  55.7 us (13%)
  starting transfers between devices  38.2 us (9%)
  other arithmetic  17.8 us (4%)
    all_to_all x1, blocking collectives, shards(): lax.all_to_all(outgoing, ('req', 'exp'), split_axis=0, concat_axis=0, til...  58.8 us
    all_to_all x1, waiting for transfers between devices, shards(): lax.all_to_all(mixed_part.astype(jnp.bfloat16).reshape(exp_count, tok_row...  55.1 us
    all_to_all x1, waiting for transfers between devices, shards(): lax.all_to_all(shared_part.reshape(exp_count, tok_rows, model_width), 'ex...  46.4 us
    all_to_all x1, waiting for transfers between devices, shards(): lax.all_to_all(answered, ('req', 'exp'), split_axis=0, concat_axis=0, til...  36.4 us
    all_to_all x1, waiting for transfers between devices, gather_exp(): got = lax.all_to_all(spread, 'exp', 0, 0, tiled=True)  24.1 us
    dot_general x1, matrix products, expert_block(): jnp.dot(hidden, down_w, preferred_element_type=jnp.float32)  16.9 us
    all_to_all x1, waiting for transfers between devices, shards(): lax.all_to_all(cache_key.reshape(key_count, HEADS, HEAD_DIM).transpose(1,...  14 us
    dot_general x1, matrix products, shards(): jnp.dot(attention, out_proj, preferred_element_type=jnp.float32)  12.3 us
  transfers between devices with their start and end apart: 7, of which 6 were waited for; matrix products, arithmetic and copies ran while one was open for 22% of the time, Pallas kernels for 0%

profile of v2, /device:TPU:0, one launch (start us, length us, event | category | flops | bytes accessed | tf_op | source)
XLA Modules:
  0.0 412.4 jit_solution(17603031507974424341)
XLA Ops:
  0.0 1.1 copy.50
  1.1 0.8 copy.42
  1.9 8.0 %all-to-all-start = ((bf16[16,64,128]{2,1,0:T(8,128)(2,1)}), bf16[16,64,128]{2,1,0:T(8,128)(2,1)S(1)}, u32[]{:S(2)}, u32[]{:S(2)}) async-start(bf16[16,64,128]{2,1,0:T(8,128)(2,1)} %copy.42), calls=%async_computation | async-start | bytes 524288 | tf_op jit(solution)/shard_map/all_to_all | solution.py:64
  9.9 1.5 copy.51
  11.4 0.0 copy-start.17
  11.4 1.3 copy.43
  12.6 6.0 %all-to-all-done = bf16[16,64,128]{2,1,0:T(8,128)(2,1)S(1)} async-done(((bf16[16,64,128]{2,1,0:T(8,128)(2,1)}), bf16[16,64,128]{2,1,0:T(8,128)(2,1)S(1)}, u32[]{:S(2)}, u32[]{:S(2)}) %all-to-all-start) | async-done | bytes 262176 | tf_op jit(solution)/shard_map/all_to_all | solution.py:64
  18.6 0.7 copy-done.4
  19.3 3.7 all-to-all-start.1
  23.0 0.2 copy.52
  23.2 1.3 copy.44
  24.5 0.1 select_reduce_fusion.2
  24.6 0.7 add_bitcast_fusion
  25.2 14.0 %all-to-all-done.1 = bf16[16,256,128]{2,1,0:T(8,128)(2,1)S(1)} async-done(((bf16[16,256,128]{2,1,0:T(8,128)(2,1)}), bf16[16,256,128]{2,1,0:T(8,128)(2,1)S(1)}, u32[]{:S(2)}, u32[]{:S(2)}) %all-to-all-start.1) | async-done | bytes 1048608 | tf_op jit(solution)/shard_map/all_to_all | solution.py:69
  39.2 3.7 all-to-all-start.2
  42.9 0.0 copy-start.9
  42.9 0.0 copy-start.11
  42.9 6.1 %fusion = (f32[1024]{0:T(1024)S(1)}, f32[1024,4096]{1,0:T(8,128)S(1)}) fusion(s32[4096]{0:T(1024)S(1)} %get-tuple-element.11, s32[4096]{0:T(1024)} %get-tuple-element.12, s32[1024]{0:T(1024)} %param.25, s32[1024]{0:T(1024)} %param.24, bf16[1024,128]{1,0:T(8,128)(2,1)} %bitcast.87, bf16[4096,128]{1,0:T(8,128)(2,1)S(1)} %bitcast.81), kind=kOutput, calls=%fused_computation.5 | convolution fusion | flops 1098906624 | bytes 18132992 | tf_op jit(solution)/shard_map/dot_general | solution.py:88
  49.0 5.7 %copy-done.1 = f32[1024,4096]{1,0:T(8,128)} copy-done((f32[1024,4096]{1,0:T(8,128)}, f32[1024,4096]{1,0:T(8,128)S(1)}, u32[]{:S(2)}) %copy-start.1) | copy-done | bytes 16777240
  54.7 0.4 copy-done.13
  55.2 0.0 copy-start.12
  55.2 0.0 copy-start.18
  55.2 6.1 %fusion.1 = f32[1024]{0:T(1024)S(1)} fusion(f32[1024,4096]{1,0:T(8,128)S(1)} %get-tuple-element.10, f32[1024]{0:T(1024)S(1)} %get-tuple-element.9, s32[4096]{0:T(1024)S(1)} %get-tuple-element.11, s32[4096]{0:T(1024)S(1)} %copy-done.6, s32[1024]{0:T(1024)S(1)} %copy-done.9, s32[1024]{0:T(1024)S(1)} %copy-done.11), kind=kLoop, calls=%fused_computation.6 | loop fusion | flops 33553408 | bytes 16826368 | tf_op jit(solution)/shard_map/reduce_sum | solution.py:94
  61.3 12.3 %convolution_convert_fusion.1 = bf16[1024,2048]{1,0:T(8,128)(2,1)} fusion(bf16[128,2048]{1,0:T(8,128)(2,1)S(1)} %copy-done.18, bf16[4096,128]{1,0:T(8,128)(2,1)S(1)} %bitcast.82, f32[1024,4096]{1,0:T(8,128)} %copy-done.1, f32[1024]{0:T(1024)} %copy-done.13, s32[4096]{0:T(1024)S(1)} %get-tuple-element.11, s32[4096]{0:T(1024)S(1)} %copy-done.7, ...), kind=kOutput, calls=%fused_computation.19 | convolution fusion | flops 1646526464 | bytes 22593536 | tf_op jit(solution)/shard_map/dot_general | solution.py:99
  73.6 7.4 %all-to-all-start.3 = ((bf16[16,64,2048]{2,1,0:T(8,128)(2,1)}), bf16[16,64,2048]{2,1,0:T(8,128)(2,1)}, u32[]{:S(2)}, u32[]{:S(2)}) async-start(bf16[16,64,2048]{2,1,0:T(8,128)(2,1)} %bitcast.75), calls=%async_computation.3 | async-start | bytes 8388608 | tf_op jit(solution)/shard_map/all_to_all | solution.py:101
  81.0 0.0 copy-start.2
  81.0 0.8 constant_dynamic-slice_fusion
  81.8 0.1 copy.45
  81.9 0.1 eq.93
  82.0 0.1 eq.84
  82.1 0.1 copy.47
  82.2 0.2 convert_reduce_fusion.2
  82.4 0.2 fusion.35
  82.7 0.2 select_reduce_fusion
  83.0 55.1 %all-to-all-done.3 = bf16[16,64,2048]{2,1,0:T(8,128)(2,1)} async-done(((bf16[16,64,2048]{2,1,0:T(8,128)(2,1)}), bf16[16,64,2048]{2,1,0:T(8,128)(2,1)}, u32[]{:S(2)}, u32[]{:S(2)}) %all-to-all-start.3) | async-done | bytes 4194336 | tf_op jit(solution)/shard_map/all_to_all | solution.py:101
  138.1 3.0 convert_reduce_fusion.1
  141.1 0.2 multiply_reduce_fusion.1
  141.3 0.1 multiply_convert_fusion.1
  141.5 0.5 broadcast_in_dim.30
  142.0 1.1 reshape.169
  143.1 5.0 %scatter_custom_fusion = bf16[768,2048]{1,0:T(8,128)(2,1)} fusion(s32[256]{0:T(256)S(1)} %bitcast.89, bf16[256,2048]{1,0:T(8,128)(2,1)} %reshape.169, bf16[]{:T(256)} %constant.16.clone.1), kind=kCustom, calls=%fused_computation.22 | custom fusion | bytes 3146240 | tf_op jit(solution)/shard_map/scatter | solution.py:145
  148.1 6.3 %reshape.152 = bf16[128,6,2048]{2,1,0:T(8,128)(2,1)} reshape(bf16[768,2048]{1,0:T(8,128)(2,1)} %scatter_custom_fusion) | data formatting | bytes 6291456 | tf_op jit(solution)/shard_map/reshape | solution.py:147
  154.3 58.8 %all_to_all.40 = bf16[128,6,2048]{2,1,0:T(8,128)(2,1)} all-to-all(bf16[128,6,2048]{2,1,0:T(8,128)(2,1)} %reshape.152), channel_id=1, replica_groups=mesh['req'=8,'exp'=16] {'req','exp'}, dimensions={0} | all-to-all | bytes 6291456 | tf_op jit(solution)/shard_map/all_to_all | solution.py:148
  213.1 2.5 broadcast_in_dim.26
  215.6 4.8 %all-to-all-start.4 = ((bf16[16,64,2048]{2,1,0:T(8,128)(2,1)}), bf16[16,64,2048]{2,1,0:T(8,128)(2,1)}, u32[]{:S(2)}, u32[]{:S(2)}) async-start(bf16[16,64,2048]{2,1,0:T(8,128)(2,1)} %broadcast_in_dim.26), calls=%async_computation.4 | async-start | bytes 8388608 | tf_op jit(solution)/shard_map/all_to_all | solution.py:25
  220.4 6.3 %reshape.153 = bf16[768,2048]{1,0:T(8,128)(2,1)} reshape(bf16[128,6,2048]{2,1,0:T(8,128)(2,1)} %all_to_all.40) | data formatting | bytes 6291456 | tf_op jit(solution)/shard_map/reshape | solution.py:150
  226.8 9.7 %fusion.7 = f32[768,1408]{1,0:T(8,128)} fusion(bf16[768,2048]{1,0:T(8,128)(2,1)} %reshape.153, bf16[1,2048,1408]{2,1,0:T(8,128)(2,1)} %param.29), kind=kOutput, calls=%fused_computation.13 | convolution fusion | flops 4429185024 | bytes 13238272 | tf_op jit(solution)/shard_map/dot_general | solution.py:13
  236.4 16.9 %fusion.13 = bf16[768,2048]{1,0:T(8,128)(2,1)} fusion(bf16[1,1408,2048]{2,1,0:T(8,128)(2,1)} %param.30, f32[768,1408]{1,0:T(8,128)} %fusion.7, bf16[768,2048]{1,0:T(8,128)(2,1)} %reshape.153, bf16[1,2048,1408]{2,1,0:T(8,128)(2,1)} %param.28), kind=kOutput, calls=%fused_computation.20 | convolution fusion | flops 8866430976 | bytes 22151168 | tf_op jit(solution)/shard_map/dot_general | solution.py:15
  253.3 6.3 %reshape.154 = bf16[128,6,2048]{2,1,0:T(8,128)(2,1)} reshape(bf16[768,2048]{1,0:T(8,128)(2,1)} %fusion.13) | data formatting | bytes 6291456 | tf_op jit(solution)/shard_map/reshape | solution.py:151
  259.6 24.1 %all-to-all-done.4 = bf16[16,64,2048]{2,1,0:T(8,128)(2,1)} async-done(((bf16[16,64,2048]{2,1,0:T(8,128)(2,1)}), bf16[16,64,2048]{2,1,0:T(8,128)(2,1)}, u32[]{:S(2)}, u32[]{:S(2)}) %all-to-all-start.4) | async-done | bytes 4194336 | tf_op jit(solution)/shard_map/all_to_all | solution.py:25
  283.7 5.9 %all-to-all-start.7 = ((bf16[128,6,2048]{2,1,0:T(8,128)(2,1)}), bf16[128,6,2048]{2,1,0:T(8,128)(2,1)}, u32[]{:S(2)}, u32[]{:S(2)}) async-start(bf16[128,6,2048]{2,1,0:T(8,128)(2,1)} %reshape.154), calls=%async_computation.7 | async-start | bytes 8388608 | tf_op jit(solution)/shard_map/all_to_all | solution.py:152
  289.6 5.4 %fusion.49 = f32[1024,352]{0,1:T(8,128)} fusion(bf16[1024,2048]{1,0:T(8,128)(2,1)} %bitcast.10, bf16[2048,352]{0,1:T(8,128)(2,1)} %param.31), kind=kOutput, calls=%fused_computation.70 | convolution fusion | flops 1476395008 | bytes 7077888 | tf_op jit(solution)/shard_map/dot_general | solution.py:111
  295.0 8.9 %convolution_convert_fusion = bf16[1024,2048]{1,0:T(8,128)(2,1)} fusion(bf16[352,2048]{1,0:T(8,128)(2,1)S(1)} %copy-done, bf16[1024,2048]{1,0:T(8,128)(2,1)} %bitcast.10, bf16[2048,352]{0,1:T(8,128)(2,1)} %param.32, f32[1024,352]{0,1:T(8,128)} %fusion.49), kind=kOutput, calls=%fused_computation.18 | convolution fusion | flops 2957049856 | bytes 12713984 | tf_op jit(solution)/shard_map/dot_general | solution.py:114
  304.0 36.4 %all-to-all-done.7 = bf16[128,6,2048]{2,1,0:T(8,128)(2,1)} async-done(((bf16[128,6,2048]{2,1,0:T(8,128)(2,1)}), bf16[128,6,2048]{2,1,0:T(8,128)(2,1)}, u32[]{:S(2)}, u32[]{:S(2)}) %all-to-all-start.7) | async-done | bytes 3145760 | tf_op jit(solution)/shard_map/all_to_all | solution.py:152
  340.3 4.9 %all-to-all-start.5 = ((bf16[16,64,2048]{2,1,0:T(8,128)(2,1)}), bf16[16,64,2048]{2,1,0:T(8,128)(2,1)}, u32[]{:S(2)}, u32[]{:S(2)}) async-start(bf16[16,64,2048]{2,1,0:T(8,128)(2,1)} %bitcast.76), calls=%async_computation.5 | async-start | bytes 8388608 | tf_op jit(solution)/shard_map/all_to_all | solution.py:118
  345.3 0.7 copy.49
  346.0 0.2 fusion.22
  346.2 6.4 %reshape.155 = bf16[768,2048]{1,0:T(8,128)(2,1)} reshape(bf16[128,6,2048]{2,1,0:T(8,128)(2,1)} %all-to-all-done.7) | data formatting | bytes 6291456 | tf_op jit(solution)/shard_map/reshape | solution.py:154
  352.6 4.7 %gather_fusion = bf16[256,2048]{1,0:T(8,128)(2,1)S(1)} fusion(bf16[768,2048]{1,0:T(8,128)(2,1)} %reshape.155, s32[1024]{0:T(1024)S(1)} %pad_clamp_fusion), kind=kCustom, calls=%fused_computation | custom fusion | bytes 2098176 | tf_op jit(solution)/shard_map/gather | solution.py:155
  357.2 1.7 reshape.156
  359.0 3.2 multiply_reduce_fusion
  362.1 46.4 %all-to-all-done.5 = bf16[16,64,2048]{2,1,0:T(8,128)(2,1)} async-done(((bf16[16,64,2048]{2,1,0:T(8,128)(2,1)}), bf16[16,64,2048]{2,1,0:T(8,128)(2,1)}, u32[]{:S(2)}, u32[]{:S(2)}) %all-to-all-start.5) | async-done | bytes 4194336 | tf_op jit(solution)/shard_map/all_to_all | solution.py:118
  408.6 3.0 convert_reduce_fusion
  411.6 0.8 add_convert_fusion
  (43 shorter events, 0.2 us)
Async XLA Ops:
  0.0 295.0 %copy-start = (bf16[352,2048]{1,0:T(8,128)(2,1)S(1)}, bf16[352,2048]{1,0:T(8,128)(2,1)}, u32[]{:S(2)}) copy-start(bf16[352,2048]{1,0:T(8,128)(2,1)} %param.33) | copy-start | bytes 4325380
  0.0 22.9 %copy-start.3 = (bf16[2,128,2048]{2,1,0:T(8,128)(2,1)S(1)}, bf16[2,128,2048]{2,1,0:T(8,128)(2,1)}, u32[]{:S(2)}) copy-start(bf16[2,128,2048]{2,1,0:T(8,128)(2,1)} %param.22) | copy-start | bytes 3145732
  1.9 16.7 %all-to-all-start = ((bf16[16,64,128]{2,1,0:T(8,128)(2,1)}), bf16[16,64,128]{2,1,0:T(8,128)(2,1)S(1)}, u32[]{:S(2)}, u32[]{:S(2)}) async-start(bf16[16,64,128]{2,1,0:T(8,128)(2,1)} %copy.42), calls=%async_computation | async-start | bytes 524288 | tf_op jit(solution)/shard_map/all_to_all | solution.py:64
  11.4 13.1 %copy-start.17 = (s32[4,8]{1,0:T(4,128)S(1)}, s32[4,8]{1,0:T(4,128)}, u32[]{:S(2)}) copy-start(s32[4,8]{1,0:T(4,128)} %param.23) | copy-start | bytes 388
  18.6 0.7 copy-start.4
  19.3 20.0 %all-to-all-start.1 = ((bf16[16,256,128]{2,1,0:T(8,128)(2,1)}), bf16[16,256,128]{2,1,0:T(8,128)(2,1)S(1)}, u32[]{:S(2)}, u32[]{:S(2)}) async-start(bf16[16,256,128]{2,1,0:T(8,128)(2,1)} %copy.43), calls=%async_computation.1 | async-start | bytes 2097152 | tf_op jit(solution)/shard_map/all_to_all | solution.py:69
  39.2 22.0 %all-to-all-start.2 = ((bf16[16,256,128]{2,1,0:T(8,128)(2,1)}), bf16[16,256,128]{2,1,0:T(8,128)(2,1)S(1)}, u32[]{:S(2)}, u32[]{:S(2)}) async-start(bf16[16,256,128]{2,1,0:T(8,128)(2,1)} %copy.44), calls=%async_computation.2 | async-start | bytes 2097152 | tf_op jit(solution)/shard_map/all_to_all | solution.py:72
  42.9 12.2 %copy-start.6 = (s32[4096]{0:T(1024)S(1)}, s32[4096]{0:T(1024)}, u32[]{:S(2)}) copy-start(s32[4096]{0:T(1024)} %get-tuple-element.12) | copy-start | bytes 49156
  42.9 12.2 %copy-start.9 = (s32[1024]{0:T(1024)S(1)}, s32[1024]{0:T(1024)}, u32[]{:S(2)}) copy-start(s32[1024]{0:T(1024)} %param.25) | copy-start | bytes 12292
  42.9 12.2 %copy-start.11 = (s32[1024]{0:T(1024)S(1)}, s32[1024]{0:T(1024)}, u32[]{:S(2)}) copy-start(s32[1024]{0:T(1024)} %param.24) | copy-start | bytes 12292
  49.0 5.7 %copy-start.1 = (f32[1024,4096]{1,0:T(8,128)}, f32[1024,4096]{1,0:T(8,128)S(1)}, u32[]{:S(2)}) copy-start(f32[1024,4096]{1,0:T(8,128)S(1)} %get-tuple-element.10) | copy-start | bytes 50331652
  49.0 6.1 %copy-start.13 = (f32[1024]{0:T(1024)}, f32[1024]{0:T(1024)S(1)}, u32[]{:S(2)}) copy-start(f32[1024]{0:T(1024)S(1)} %get-tuple-element.9) | copy-start | bytes 12292
  55.1 6.1 %copy-start.7 = (s32[4096]{0:T(1024)S(1)}, s32[4096]{0:T(1024)}, u32[]{:S(2)}) copy-start(s32[4096]{0:T(1024)} %get-tuple-element.12) | copy-start | bytes 49156
  55.2 6.1 %copy-start.10 = (s32[1024]{0:T(1024)S(1)}, s32[1024]{0:T(1024)}, u32[]{:S(2)}) copy-start(s32[1024]{0:T(1024)} %param.25) | copy-start | bytes 12292
  55.2 6.1 %copy-start.12 = (s32[1024]{0:T(1024)S(1)}, s32[1024]{0:T(1024)}, u32[]{:S(2)}) copy-start(s32[1024]{0:T(1024)} %param.24) | copy-start | bytes 12292
  55.2 6.1 %copy-start.18 = (bf16[128,2048]{1,0:T(8,128)(2,1)S(1)}, bf16[128,2048]{1,0:T(8,128)(2,1)}, u32[]{:S(2)}) copy-start(bf16[128,2048]{1,0:T(8,128)(2,1)} %param.26) | copy-start | bytes 1572868
  73.6 8.6 %copy-start.15 = (s32[128]{0:T(128)S(1)}, s32[128]{0:T(128)}, u32[]{:S(2)}) copy-start(s32[128]{0:T(128)} %param.35) | copy-start | bytes 1540
  73.6 64.5 %all-to-all-start.3 = ((bf16[16,64,2048]{2,1,0:T(8,128)(2,1)}), bf16[16,64,2048]{2,1,0:T(8,128)(2,1)}, u32[]{:S(2)}, u32[]{:S(2)}) async-start(bf16[16,64,2048]{2,1,0:T(8,128)(2,1)} %bitcast.75), calls=%async_computation.3 | async-start | bytes 8388608 | tf_op jit(solution)/shard_map/all_to_all | solution.py:101
  81.0 60.2 %copy-start.2 = (bf16[64,2048]{1,0:T(8,128)(2,1)S(1)}, bf16[64,2048]{1,0:T(8,128)(2,1)}, u32[]{:S(2)}) copy-start(bf16[64,2048]{1,0:T(8,128)(2,1)} %param.19) | copy-start | bytes 786436
  81.0 60.4 %copy-start.8 = (f32[2048]{0:T(1024)S(1)}, f32[2048]{0:T(1024)}, u32[]{:S(2)}) copy-start(f32[2048]{0:T(1024)} %param.27) | copy-start | bytes 24580
  215.6 68.1 %all-to-all-start.4 = ((bf16[16,64,2048]{2,1,0:T(8,128)(2,1)}), bf16[16,64,2048]{2,1,0:T(8,128)(2,1)}, u32[]{:S(2)}, u32[]{:S(2)}) async-start(bf16[16,64,2048]{2,1,0:T(8,128)(2,1)} %broadcast_in_dim.26), calls=%async_computation.4 | async-start | bytes 8388608 | tf_op jit(solution)/shard_map/all_to_all | solution.py:25
  283.7 56.6 %all-to-all-start.7 = ((bf16[128,6,2048]{2,1,0:T(8,128)(2,1)}), bf16[128,6,2048]{2,1,0:T(8,128)(2,1)}, u32[]{:S(2)}, u32[]{:S(2)}) async-start(bf16[128,6,2048]{2,1,0:T(8,128)(2,1)} %reshape.154), calls=%async_computation.7 | async-start | bytes 8388608 | tf_op jit(solution)/shard_map/all_to_all | solution.py:152
  340.3 5.0 %copy-start.16 = (f32[64,4]{0,1:T(4,128)S(1)}, f32[64,4]{0,1:T(4,128)}, u32[]{:S(2)}) copy-start(f32[64,4]{0,1:T(4,128)} %param.37) | copy-start | bytes 3076
  340.3 5.7 %copy-start.14 = (bf16[2048]{0:T(1024)(128)(2,1)S(1)}, bf16[2048]{0:T(1024)(128)(2,1)}, u32[]{:S(2)}) copy-start(bf16[2048]{0:T(1024)(128)(2,1)} %param.34) | copy-start | bytes 12292
  340.3 68.3 %all-to-all-start.5 = ((bf16[16,64,2048]{2,1,0:T(8,128)(2,1)}), bf16[16,64,2048]{2,1,0:T(8,128)(2,1)}, u32[]{:S(2)}, u32[]{:S(2)}) async-start(bf16[16,64,2048]{2,1,0:T(8,128)(2,1)} %bitcast.76), calls=%async_computation.5 | async-start | bytes 8388608 | tf_op jit(solution)/shard_map/all_to_all | solution.py:118
  352.6 6.4 %copy-start.5 = (f32[64,4]{1,0:T(8,128)S(1)}, f32[64,4]{1,0:T(8,128)}, u32[]{:S(2)}) copy-start(f32[64,4]{1,0:T(8,128)} %copy.49) | copy-start | bytes 3076
